TPU v7x, 512 devices: a whole 4x8x8 slice. The times are simulated.
512 devices in a mesh: rows: 16 (over x_lo, z), cols: 32 (over y, x_hi, core).
Axes of the slice: x: 4 (x_hi: 2, x_lo: 2; x = x_hi * 2 + x_lo), y: 8, z: 8, core: 2. Of those that a mesh axis runs over, the one named last changes fastest.
Arguments:
- tokens: bfloat16 [128, 1024, 192], P('rows', 'cols'), may hold values from -60 to 60
- region_ids: int32 [128, 1024], P('rows', 'cols'), may hold values from 0 to 2
- upper_rim: bfloat16 [4, 1024, 192], P(None, 'cols'), may hold values from -60 to 60
- upper_ids: int32 [4, 1024], P(None, 'cols'), may hold values from 0 to 2
- lower_rim: bfloat16 [4, 1024, 192], P(None, 'cols'), may hold values from -60 to 60
- lower_ids: int32 [4, 1024], P(None, 'cols'), may hold values from 0 to 2
- cotangent: bfloat16 [128, 1024, 192], P('rows', 'cols'), may hold values from -6 to 6
- qkv_weight: bfloat16 [2, 192, 576], replicated, may hold values from -0.4375 to 0.4375
- proj_weight: bfloat16 [2, 192, 192], replicated, may hold values from -0.4375 to 0.4375
- inner_weight: bfloat16 [2, 192, 768], replicated, may hold values from -0.4375 to 0.4375
- outer_weight: bfloat16 [2, 768, 192], replicated, may hold values from -0.21875 to 0.21875
- bias_table: float32 [2, 225, 6], replicated, may hold values from -4 to 400
Outputs:
- token_grad: bfloat16 [128, 1024, 192], P('rows', 'cols')
- qkv_grad: float32 [2, 192, 576], P(None, 'rows', 'cols')
- proj_grad: float32 [2, 192, 192], P(None, 'rows', 'cols')
- inner_grad: float32 [2, 192, 768], P(None, 'rows', 'cols')
- outer_grad: float32 [2, 768, 192], P(None, 'rows', 'cols')
- table_grad: float32 [2, 225, 6], replicated
All inputs are finite; a program needn't handle non-finite values.
Results may differ from a plain program's by a relative error of at most 0.03.
Values may be sent and summed in bfloat16 or wider, within the bound.
A program may use at most 64 MiB of HBM per device.

v0:
```python
import jax
import jax.numpy as jnp
from jax import lax
from jax.sharding import PartitionSpec as P

WIN = 8
HALF = 4
BIAS_LEN = 225
EPS = 1e-05
MASKED = -1000000000.0


def with_halo(block, sides, width, periodic):
    for axis, dim in sides:
        count = lax.axis_size(axis)
        forward = [(i, i + 1) for i in range(count - 1)]
        if periodic:
            forward.append((count - 1, 0))
        backward = [(target, source) for source, target in forward]
        low = lax.ppermute(
            lax.slice_in_dim(block, block.shape[dim] - width, None, axis=dim), axis, forward
        )
        high = lax.ppermute(lax.slice_in_dim(block, 0, width, axis=dim), axis, backward)
        block = jnp.concatenate([low, block, high], axis=dim)
    return block


def normalize(values):
    center = jnp.mean(values, axis=-1, keepdims=True)
    shifted = values - center
    spread = jnp.mean(shifted * shifted, axis=-1, keepdims=True)
    return shifted * lax.rsqrt(spread + EPS)


def norm_back(source, grad_norm):
    _, pullback = jax.vjp(normalize, source.astype(jnp.float32))
    return pullback(grad_norm)[0]


def by_transpose(left, right):
    return lax.dot_general(
        left, right, (((1,), (1,)), ((), ())), preferred_element_type=jnp.float32
    )


def over_rows(left, right):
    return lax.dot_general(
        left, right, (((0,), (0,)), ((), ())), preferred_element_type=jnp.float32
    )


def windows(surface):
    grid_rows, grid_cols = (surface.shape[0], surface.shape[1])
    trailing = surface.shape[2:]
    blocked = surface.reshape((grid_rows // WIN, WIN, grid_cols // WIN, WIN) + trailing)
    permute = (0, 2, 1, 3) + tuple(range(4, 4 + len(trailing)))
    return blocked.transpose(permute).reshape(
        (grid_rows // WIN * (grid_cols // WIN), WIN * WIN) + trailing
    )


def unwindows(framed, grid_rows, grid_cols):
    trailing = framed.shape[2:]
    blocked = framed.reshape((grid_rows // WIN, grid_cols // WIN, WIN, WIN) + trailing)
    permute = (0, 2, 1, 3) + tuple(range(4, 4 + len(trailing)))
    return blocked.transpose(permute).reshape((grid_rows, grid_cols) + trailing)


def relative_onehot():
    places = jnp.arange(WIN * WIN, dtype=jnp.int32)
    pos_row = places // WIN
    pos_col = places % WIN
    lookup = (
        (pos_row[:, None] - pos_row[None, :] + WIN - 1) * (2 * WIN - 1)
        + pos_col[:, None]
        - pos_col[None, :]
        + WIN
        - 1
    )
    return (lookup[:, :, None] == jnp.arange(BIAS_LEN, dtype=jnp.int32)[None, None, :]).astype(
        jnp.float32
    )


def attend(normed_win, ids_win, qkv_weight, pos_bias):
    window_count, window_size, channels = normed_win.shape
    head_count = pos_bias.shape[0]
    head_size = channels // head_count
    score_scale = head_size ** (-0.5)
    qkv_all = jnp.dot(
        normed_win.reshape(window_count * window_size, channels),
        qkv_weight,
        preferred_element_type=jnp.float32,
    )
    qkv_all = qkv_all.astype(jnp.bfloat16).reshape(
        window_count, window_size, 3, head_count, head_size
    )
    scores = jnp.einsum(
        "nqhd,nkhd->nhqk", qkv_all[:, :, 0], qkv_all[:, :, 1], preferred_element_type=jnp.float32
    )
    scores = scores * score_scale + pos_bias[None]
    same_region = ids_win[:, :, None] == ids_win[:, None, :]
    scores = jnp.where(same_region[:, None], scores, MASKED)
    row_max = jnp.max(scores, axis=-1, keepdims=True)
    exponent = jnp.exp(scores - row_max)
    attn_probs = exponent / jnp.sum(exponent, axis=-1, keepdims=True)
    attn_out = jnp.einsum(
        "nhqk,nkhd->nqhd",
        attn_probs.astype(jnp.bfloat16),
        qkv_all[:, :, 2],
        preferred_element_type=jnp.float32,
    )
    return (
        qkv_all,
        attn_probs,
        attn_out.astype(jnp.bfloat16).reshape(window_count, window_size, channels),
    )


def attend_back(normed_win, qkv_all, attn_probs, grad_out, qkv_weight):
    window_count, window_size, channels = normed_win.shape
    head_count, head_size = (qkv_all.shape[3], qkv_all.shape[4])
    score_scale = head_size ** (-0.5)
    grad_heads = grad_out.reshape(window_count, window_size, head_count, head_size)
    grad_probs = jnp.einsum(
        "nqhd,nkhd->nhqk", grad_heads, qkv_all[:, :, 2], preferred_element_type=jnp.float32
    )
    grad_scores = attn_probs * (
        grad_probs - jnp.sum(grad_probs * attn_probs, axis=-1, keepdims=True)
    )
    grad_bias = jnp.sum(grad_scores, axis=0)
    scores_low = grad_scores.astype(jnp.bfloat16)
    grad_query = (
        jnp.einsum(
            "nhqk,nkhd->nqhd", scores_low, qkv_all[:, :, 1], preferred_element_type=jnp.float32
        )
        * score_scale
    )
    grad_key = (
        jnp.einsum(
            "nhqk,nqhd->nkhd", scores_low, qkv_all[:, :, 0], preferred_element_type=jnp.float32
        )
        * score_scale
    )
    grad_value = jnp.einsum(
        "nhqk,nqhd->nkhd",
        attn_probs.astype(jnp.bfloat16),
        grad_heads,
        preferred_element_type=jnp.float32,
    )
    grad_qkv = jnp.stack([grad_query, grad_key, grad_value], axis=2).astype(jnp.bfloat16)
    grad_qkv = grad_qkv.reshape(window_count * window_size, 3 * channels)
    flattened = normed_win.reshape(window_count * window_size, channels)
    grad_norm = by_transpose(grad_qkv, qkv_weight)
    grad_weight = over_rows(flattened, grad_qkv)
    return (grad_norm.reshape(window_count, window_size, channels), grad_weight, grad_bias)


def mixer_forward(surface, region, qkv_weight, table):
    grid_rows, grid_cols = (surface.shape[0], surface.shape[1])
    normed = normalize(surface.astype(jnp.float32)).astype(jnp.bfloat16)
    pos_bias = jnp.einsum("ijb,bh->hij", relative_onehot(), table, precision=lax.Precision.HIGHEST)
    qkv_all, attn_probs, attn_out = attend(windows(normed), windows(region), qkv_weight, pos_bias)
    return (normed, qkv_all, attn_probs, unwindows(attn_out, grid_rows, grid_cols))


def mixer_backward(surface, normed, qkv_all, attn_probs, grad_mix, qkv_weight):
    grid_rows, grid_cols = (surface.shape[0], surface.shape[1])
    grad_norm, grad_weight, grad_bias = attend_back(
        windows(normed), qkv_all, attn_probs, windows(grad_mix), qkv_weight
    )
    grad_surface = norm_back(surface, unwindows(grad_norm, grid_rows, grid_cols))
    grad_table = jnp.einsum(
        "ijb,hij->bh", relative_onehot(), grad_bias, precision=lax.Precision.HIGHEST
    )
    return (grad_surface, grad_weight, grad_table)


def channel_forward(middle, inner_w, outer_w):
    normed = normalize(middle.astype(jnp.float32)).astype(jnp.bfloat16)
    hidden_pre = jnp.dot(normed, inner_w, preferred_element_type=jnp.float32)
    hidden_act = jax.nn.gelu(hidden_pre, approximate=False).astype(jnp.bfloat16)
    output = (
        middle.astype(jnp.float32)
        + jnp.dot(hidden_act, outer_w, preferred_element_type=jnp.float32)
    ).astype(jnp.bfloat16)
    return (normed, hidden_pre, hidden_act, output)


def channel_backward(middle, normed, hidden_pre, hidden_act, grad_out, inner_w, outer_w):
    grad_act = by_transpose(grad_out, outer_w)
    grad_outer = over_rows(hidden_act, grad_out)
    _, pullback = jax.vjp(lambda inputs: jax.nn.gelu(inputs, approximate=False), hidden_pre)
    grad_pre = pullback(grad_act)[0].astype(jnp.bfloat16)
    grad_norm = by_transpose(grad_pre, inner_w)
    grad_inner = over_rows(normed, grad_pre)
    grad_middle = (grad_out.astype(jnp.float32) + norm_back(middle, grad_norm)).astype(jnp.bfloat16)
    return (grad_middle, grad_inner, grad_outer)


def fold_rims(grad_ext):
    col_edges = jnp.concatenate([grad_ext[:, :HALF], grad_ext[:, -HALF:]], axis=1)
    col_recv = with_halo(col_edges.astype(jnp.bfloat16), (("cols", 1),), HALF, True).astype(
        col_edges.dtype
    )
    center = grad_ext[:, HALF:-HALF]
    center = jnp.concatenate(
        [
            center[:, :HALF] + col_recv[:, :HALF],
            center[:, HALF:-HALF],
            center[:, -HALF:] + col_recv[:, -HALF:],
        ],
        axis=1,
    )
    row_edges = jnp.concatenate([center[:HALF], center[-HALF:]], axis=0)
    row_recv = with_halo(row_edges.astype(jnp.bfloat16), (("rows", 0),), HALF, False).astype(
        row_edges.dtype
    )
    interior = center[HALF:-HALF]
    return jnp.concatenate(
        [
            interior[:HALF] + row_recv[:HALF],
            interior[HALF:-HALF],
            interior[-HALF:] + row_recv[-HALF:],
        ],
        axis=0,
    )


def reduce_grads(qkv_term, proj_term, inner_term, outer_term):
    row_count = lax.axis_size("rows")
    col_count = lax.axis_size("cols")
    tile_count = row_count * col_count
    reduced = (
        lax.psum_scatter(
            qkv_term.astype(jnp.bfloat16), "cols", scatter_dimension=1, tiled=True
        ).astype(jnp.float32),
        lax.psum_scatter(
            proj_term.astype(jnp.bfloat16), "cols", scatter_dimension=1, tiled=True
        ).astype(jnp.float32),
        lax.psum_scatter(
            inner_term.astype(jnp.bfloat16), "cols", scatter_dimension=1, tiled=True
        ).astype(jnp.float32),
        lax.psum_scatter(
            outer_term.astype(jnp.bfloat16), "cols", scatter_dimension=1, tiled=True
        ).astype(jnp.float32),
    )
    reduced = (
        lax.psum_scatter(
            reduced[0].astype(jnp.bfloat16), "rows", scatter_dimension=0, tiled=True
        ).astype(jnp.float32),
        lax.psum_scatter(
            reduced[1].astype(jnp.bfloat16), "rows", scatter_dimension=0, tiled=True
        ).astype(jnp.float32),
        lax.psum_scatter(
            reduced[2].astype(jnp.bfloat16), "rows", scatter_dimension=0, tiled=True
        ).astype(jnp.float32),
        lax.psum_scatter(
            reduced[3].astype(jnp.bfloat16), "rows", scatter_dimension=0, tiled=True
        ).astype(jnp.float32),
    )
    return tuple((section / tile_count for section in reduced))


def local(
    tokens,
    region_ids,
    upper_rim,
    upper_ids,
    lower_rim,
    lower_ids,
    cotangent,
    qkv_weight,
    proj_weight,
    inner_weight,
    outer_weight,
    bias_table,
):
    tile_rows, tile_cols, channels = tokens.shape
    row_index = lax.axis_index("rows")
    row_count = lax.axis_size("rows")
    tile_count = row_count * lax.axis_size("cols")
    normed_one, qkv_one, probs_one, mix_one = mixer_forward(
        tokens, region_ids, qkv_weight[0], bias_table[0]
    )
    mix_flat_one = mix_one.reshape(tile_rows * tile_cols, channels)
    middle_one = (
        tokens.reshape(-1, channels).astype(jnp.float32)
        + jnp.dot(mix_flat_one, proj_weight[0], preferred_element_type=jnp.float32)
    ).astype(jnp.bfloat16)
    chan_one = channel_forward(middle_one, inner_weight[0], outer_weight[0])
    first_out = chan_one[3].reshape(tile_rows, tile_cols, channels)
    region_low = region_ids.astype(jnp.bfloat16)
    row_ext, row_ids = (
        with_halo(first_out, (("rows", 0),), HALF, False),
        with_halo(region_low, (("rows", 0),), HALF, False),
    )
    at_top = row_index == 0
    at_bottom = row_index == row_count - 1
    row_ext = jnp.concatenate(
        [
            jnp.where(at_top, upper_rim, row_ext[:HALF]),
            row_ext[HALF:-HALF],
            jnp.where(at_bottom, lower_rim, row_ext[-HALF:]),
        ],
        axis=0,
    )
    row_ids = jnp.concatenate(
        [
            jnp.where(at_top, upper_ids.astype(jnp.bfloat16), row_ids[:HALF]),
            row_ids[HALF:-HALF],
            jnp.where(at_bottom, lower_ids.astype(jnp.bfloat16), row_ids[-HALF:]),
        ],
        axis=0,
    )
    extended, ext_ids = (
        with_halo(row_ext, (("cols", 1),), HALF, True),
        with_halo(row_ids, (("cols", 1),), HALF, True),
    )
    ext_region = ext_ids.astype(jnp.int32)
    normed_two, qkv_two, probs_two, mix_ext = mixer_forward(
        extended, ext_region, qkv_weight[1], bias_table[1]
    )
    mix_flat_two = mix_ext[HALF : HALF + tile_rows, HALF : HALF + tile_cols].reshape(
        tile_rows * tile_cols, channels
    )
    middle_two = (
        chan_one[3].astype(jnp.float32)
        + jnp.dot(mix_flat_two, proj_weight[1], preferred_element_type=jnp.float32)
    ).astype(jnp.bfloat16)
    chan_two = channel_forward(middle_two, inner_weight[1], outer_weight[1])
    grad_out = cotangent.reshape(-1, channels)
    grad_mid_two, inner_two, outer_two = channel_backward(
        middle_two,
        chan_two[0],
        chan_two[1],
        chan_two[2],
        grad_out,
        inner_weight[1],
        outer_weight[1],
    )
    proj_two = over_rows(mix_flat_two, grad_mid_two)
    grad_mix_two = (
        by_transpose(grad_mid_two, proj_weight[1])
        .astype(jnp.bfloat16)
        .reshape(tile_rows, tile_cols, channels)
    )
    grad_mix_ext = jnp.pad(grad_mix_two, ((HALF, HALF), (HALF, HALF), (0, 0)))
    grad_ext, qkv_two_grad, table_two = mixer_backward(
        extended, normed_two, qkv_two, probs_two, grad_mix_ext, qkv_weight[1]
    )
    folded = fold_rims(grad_ext)
    grad_first = (
        grad_mid_two.reshape(tile_rows, tile_cols, channels).astype(jnp.float32) + folded
    ).astype(jnp.bfloat16)
    summed_two = reduce_grads(qkv_two_grad, proj_two, inner_two, outer_two)
    grad_mid_one, inner_one, outer_one = channel_backward(
        middle_one,
        chan_one[0],
        chan_one[1],
        chan_one[2],
        grad_first.reshape(-1, channels),
        inner_weight[0],
        outer_weight[0],
    )
    proj_one = over_rows(mix_flat_one, grad_mid_one)
    grad_mix_one = (
        by_transpose(grad_mid_one, proj_weight[0])
        .astype(jnp.bfloat16)
        .reshape(tile_rows, tile_cols, channels)
    )
    grad_tokens, qkv_one_grad, table_one = mixer_backward(
        tokens, normed_one, qkv_one, probs_one, grad_mix_one, qkv_weight[0]
    )
    token_grad = (
        grad_mid_one.reshape(tile_rows, tile_cols, channels).astype(jnp.float32) + grad_tokens
    ).astype(jnp.bfloat16)
    summed_one = reduce_grads(qkv_one_grad, proj_one, inner_one, outer_one)
    table_sum = lax.psum(jnp.stack([table_one, table_two]), ("rows", "cols"))
    qkv_grad = jnp.stack([summed_one[0], summed_two[0]])
    proj_grad = jnp.stack([summed_one[1], summed_two[1]])
    inner_grad = jnp.stack([summed_one[2], summed_two[2]])
    outer_grad = jnp.stack([summed_one[3], summed_two[3]])
    return (token_grad, qkv_grad, proj_grad, inner_grad, outer_grad, table_sum / tile_count)


def solution(mesh):
    return jax.shard_map(
        local,
        mesh=mesh,
        in_specs=(
            P("rows", "cols", None),
            P("rows", "cols"),
            P(None, "cols", None),
            P(None, "cols"),
            P(None, "cols", None),
            P(None, "cols"),
            P("rows", "cols", None),
            P(),
            P(),
            P(),
            P(),
            P(),
        ),
        out_specs=(
            P("rows", "cols", None),
            P(None, "rows", "cols"),
            P(None, "rows", "cols"),
            P(None, "rows", "cols"),
            P(None, "rows", "cols"),
            P(),
        ),
        check_vma=False,
    )
```

profile of v0, /device:TPU:16, one launch (start us, length us, event | category | flops | bytes accessed | tf_op | source)
XLA Modules:
  0.0 740.8 jit_solution(4633801604680968060)
XLA Ops:
  8.5 4.8 collective-permute-start.4
  27.7 2.9 multiply_convert_fusion.1
  33.3 5.2 collective-permute-start
  44.7 6.0 collective-permute-start.7
  52.6 4.1 collective-permute-start.2
  56.7 3.9 collective-permute-start.3
  64.6 3.2 reshape.352
  94.4 4.0 copy.147
  98.4 5.6 convert_element_type.304
  115.4 3.2 collective-permute-start.8
  118.7 4.7 collective-permute-start.9
  125.2 4.7 collective-permute-start.10
  132.0 6.0 collective-permute-done.11
  146.3 68.5 %fusion.122 = (bf16[192,24]{0,1:T(8,128)(2,1)S(1)}, bf16[192,24]{0,1:T(8,128)(2,1)S(1)}, bf16[192,8]{0,1:T(8,128)(2,1)S(1)}, bf16[192,8]{0,1:T(8,128)(2,1)S(1)},...) fusion(bf16[192,576]{0,1:T(8,128)(2,1)} %convolution_convert_fusion.9, ...), kind=kCustom, calls=%all-reduce-scatter.6 | all-reduce-scatter fusion | flops 786434 | bytes 1230848
  214.8 20.4 %collective-permute-start.51 = (bf16[768,6]{0,1:T(8,128)(2,1)S(1)}, bf16[768,6]{0,1:T(8,128)(2,1)S(1)}, u32[]{:S(2)}, u32[]{:S(2)}) collective-permute-start(bf16[768,6]{0,1:T(8,128)(2,1)S(1)} %slice.212), channel_id=1, source_target_pairs={{0,8},{1,9},{2,10},{3,11},{4,12},{5,13},{6,14},{7,15},{8,16},{9,17... | collective-permute-start | bytes 27656
  243.0 4.6 collective-permute-start.46
  268.8 3.1 collective-permute-start.54
  271.9 3.3 collective-permute-start.53
  304.3 4.6 collective-permute-start.38
  313.2 4.2 collective-permute-start.34
  321.4 104.6 %psum.7 = f32[2,225,6]{1,2,0:T(8,128)S(1)} all-reduce(f32[2,225,6]{1,2,0:T(8,128)S(1)} %pad_maximum_fusion.16), channel_id=1, replica_groups=mesh['rows'=16,'cols'=32] {'rows','cols'}, use_global_device_ids=true, to_apply=%region_40.41 | all-reduce | flops 2700 | bytes 21600 | tf_op jit(solution)/shard_map/psum | solution.py:379
  426.0 3.2 collective-permute-start.31
  431.1 4.8 collective-permute-start.29
  437.9 4.4 collective-permute-start.27
  443.7 5.6 collective-permute-start.26
  449.3 3.9 collective-permute-start.25
  465.6 3.3 collective-permute-start.18
  480.8 3.1 collective-permute-start.13
  485.9 2.9 collective-permute-done.13
  494.6 51.3 %reduce-scatter.29.cloned.1.call-done = bf16[192,24]{0,1:T(8,128)(2,1)} async-done(((bf16[192,768]{0,1:T(8,128)(2,1)}), bf16[192,24]{0,1:T(8,128)(2,1)}) %reduce-scatter.29.cloned.1.call-update) | async-done | bytes 9232 | tf_op jit(solution)/shard_map/reduce_scatter | solution.py:241
  545.9 121.3 %reduce-scatter.27.cloned.1.call-done = bf16[192,24]{0,1:T(8,128)(2,1)} async-done(((bf16[192,768]{0,1:T(8,128)(2,1)}), bf16[192,24]{0,1:T(8,128)(2,1)}) %reduce-scatter.27.cloned.1.call-update) | async-done | bytes 9232 | tf_op jit(solution)/shard_map/reduce_scatter | solution.py:241
  667.2 64.4 %all-reduce.19 = (bf16[192,18]{0,1:T(8,128)(2,1)S(1)}, bf16[192,18]{0,1:T(8,128)(2,1)S(1)}, bf16[192,6]{0,1:T(8,128)(2,1)S(1)}, bf16[192,6]{0,1:T(8,128)(2,1)S(1...) all-reduce(bf16[192,18]{0,1:T(8,128)(2,1)S(1)} %constant_dynamic-sl, ...), channel_id=5, replica_groups=mesh['rows'=16,'cols'=32] {'rows'}, use_global_device_ids=true, to_apply=%region_25.26.clone | all-reduce | flops 18432 | bytes 73728
  (448 shorter events, 182.2 us)
Async XLA Ops:
  7.2 485.2 %reduce-scatter.31.cloned.1.call-start = ((), (), s32[]{:S(2)}) async-start(), calls=%async_computation.6 | async-start | bytes 208896
  8.5 33.5 %collective-permute-start.4 = (bf16[4,32]{1,0:T(4,128)(2,1)}, bf16[4,32]{1,0:T(4,128)(2,1)}, u32[]{:S(2)}, u32[]{:S(2)}) collective-permute-start(bf16[4,32]{1,0:T(4,128)(2,1)} %get-tuple-element.76), channel_id=1, source_target_pairs={{0,32},{32,64},{64,96},{96,128},{128,160},{160,192},{192,224},{224... | collective-permute-start | bytes 776 | tf_op jit(solution)/shard_map/ppermute | solution.py:20
  13.4 28.6 %collective-permute-start.5 = (bf16[4,32]{1,0:T(4,128)(2,1)}, bf16[4,32]{1,0:T(4,128)(2,1)}, u32[]{:S(2)}, u32[]{:S(2)}) collective-permute-start(bf16[4,32]{1,0:T(4,128)(2,1)} %get-tuple-element.77), channel_id=1, source_target_pairs={{32,0},{64,32},{96,64},{128,96},{160,128},{192,160},{224,192},{256... | collective-permute-start | bytes 776 | tf_op jit(solution)/shard_map/ppermute | solution.py:23
  31.9 20.6 %collective-permute-start.1 = (bf16[4,32,192]{2,1,0:T(8,128)(2,1)S(1)}, bf16[4,32,192]{2,1,0:T(8,128)(2,1)S(1)}, u32[]{:S(2)}, u32[]{:S(2)}) collective-permute-start(bf16[4,32,192]{2,1,0:T(8,128)(2,1)S(1)} %bitcast.340), channel_id=1, source_target_pairs={{32,0},{64,32},{96,64},{128,96},{160,128},{192,160},{224,192},{256... | collective-permute-start | bytes 147464 | tf_op jit(solution)/shard_map/ppermute | solution.py:23
  33.3 19.3 %collective-permute-start = (bf16[4,32,192]{2,1,0:T(8,128)(2,1)S(1)}, bf16[4,32,192]{2,1,0:T(8,128)(2,1)S(1)}, u32[]{:S(2)}, u32[]{:S(2)}) collective-permute-start(bf16[4,32,192]{2,1,0:T(8,128)(2,1)S(1)} %bitcast.341), channel_id=1, source_target_pairs={{0,32},{32,64},{64,96},{96,128},{128,160},{160,192},{192,224},{224... | collective-permute-start | bytes 147464 | tf_op jit(solution)/shard_map/ppermute | solution.py:20
  214.8 28.2 %collective-permute-start.51 = (bf16[768,6]{0,1:T(8,128)(2,1)S(1)}, bf16[768,6]{0,1:T(8,128)(2,1)S(1)}, u32[]{:S(2)}, u32[]{:S(2)}) collective-permute-start(bf16[768,6]{0,1:T(8,128)(2,1)S(1)} %slice.212), channel_id=1, source_target_pairs={{0,8},{1,9},{2,10},{3,11},{4,12},{5,13},{6,14},{7,15},{8,16},{9,17... | collective-permute-start | bytes 27656
  235.2 16.9 %collective-permute-start.50 = (bf16[768,8]{0,1:T(8,128)(2,1)S(1)}, bf16[768,8]{0,1:T(8,128)(2,1)S(1)}, u32[]{:S(2)}, u32[]{:S(2)}) collective-permute-start(bf16[768,8]{0,1:T(8,128)(2,1)S(1)} %get-tuple-element.41), channel_id=1, source_target_pairs={{0,7},{1,8},{2,9},{3,10},{4,11},{5,12},{6,13},{7,14},{8,15},{9,16}... | collective-permute-start | bytes 36872
  237.2 16.9 %collective-permute-start.49 = (bf16[768,8]{0,1:T(8,128)(2,1)S(1)}, bf16[768,8]{0,1:T(8,128)(2,1)S(1)}, u32[]{:S(2)}, u32[]{:S(2)}) collective-permute-start(bf16[768,8]{0,1:T(8,128)(2,1)S(1)} %get-tuple-element.41), channel_id=1, source_target_pairs={{0,6},{1,7},{2,8},{3,9},{4,10},{5,11},{6,12},{7,13},{8,14},{9,15},... | collective-permute-start | bytes 36872
  239.1 16.9 %collective-permute-start.48 = (bf16[768,8]{0,1:T(8,128)(2,1)S(1)}, bf16[768,8]{0,1:T(8,128)(2,1)S(1)}, u32[]{:S(2)}, u32[]{:S(2)}) collective-permute-start(bf16[768,8]{0,1:T(8,128)(2,1)S(1)} %get-tuple-element.41), channel_id=1, source_target_pairs={{0,5},{1,6},{2,7},{3,8},{4,9},{5,10},{6,11},{7,12},{8,13},{9,14},{... | collective-permute-start | bytes 36872
  241.0 17.2 %collective-permute-start.47 = (bf16[768,8]{0,1:T(8,128)(2,1)S(1)}, bf16[768,8]{0,1:T(8,128)(2,1)S(1)}, u32[]{:S(2)}, u32[]{:S(2)}) collective-permute-start(bf16[768,8]{0,1:T(8,128)(2,1)S(1)} %get-tuple-element.41), channel_id=1, source_target_pairs={{0,4},{1,5},{2,6},{3,7},{4,8},{5,9},{6,10},{7,11},{8,12},{9,13},{1... | collective-permute-start | bytes 36872
  243.0 17.2 %collective-permute-start.46 = (bf16[768,8]{0,1:T(8,128)(2,1)S(1)}, bf16[768,8]{0,1:T(8,128)(2,1)S(1)}, u32[]{:S(2)}, u32[]{:S(2)}) collective-permute-start(bf16[768,8]{0,1:T(8,128)(2,1)S(1)} %get-tuple-element.41), channel_id=1, source_target_pairs={{0,3},{1,4},{2,5},{3,6},{4,7},{5,8},{6,9},{7,10},{8,11},{9,12},{10... | collective-permute-start | bytes 36872
  252.1 19.8 %collective-permute-start.58 = (bf16[768,8]{0,1:T(8,128)(2,1)S(1)}, bf16[768,8]{0,1:T(8,128)(2,1)S(1)}, u32[]{:S(2)}, u32[]{:S(2)}) collective-permute-start(bf16[768,8]{0,1:T(8,128)(2,1)S(1)} %get-tuple-element.40), channel_id=1, source_target_pairs={{0,7},{1,8},{2,9},{3,10},{4,11},{5,12},{6,13},{7,14},{8,15},{9,16}... | collective-permute-start | bytes 36872
  254.0 21.2 %collective-permute-start.57 = (bf16[768,8]{0,1:T(8,128)(2,1)S(1)}, bf16[768,8]{0,1:T(8,128)(2,1)S(1)}, u32[]{:S(2)}, u32[]{:S(2)}) collective-permute-start(bf16[768,8]{0,1:T(8,128)(2,1)S(1)} %get-tuple-element.40), channel_id=1, source_target_pairs={{0,6},{1,7},{2,8},{3,9},{4,10},{5,11},{6,12},{7,13},{8,14},{9,15},... | collective-permute-start | bytes 36872
  278.1 215.1 %reduce-scatter.33.cloned.1.call-start = ((), (), s32[]{:S(2)}) async-start(), calls=%async_computation.7 | async-start | bytes 208896
  284.5 261.4 %reduce-scatter.29.cloned.1.call-start = ((), (), s32[]{:S(2)}) async-start(), calls=%async_computation.5 | async-start | bytes 405504 | tf_op jit(solution)/shard_map/reduce_scatter | solution.py:241
  286.2 381.0 %reduce-scatter.27.cloned.1.call-start = ((), (), s32[]{:S(2)}) async-start(), calls=%async_computation.4 | async-start | bytes 405504 | tf_op jit(solution)/shard_map/reduce_scatter | solution.py:241
  287.5 21.5 %collective-permute-start.42 = (bf16[192,8]{0,1:T(8,128)(2,1)S(1)}, bf16[192,8]{0,1:T(8,128)(2,1)S(1)}, u32[]{:S(2)}, u32[]{:S(2)}) collective-permute-start(bf16[192,8]{0,1:T(8,128)(2,1)S(1)} %get-tuple-element.38), channel_id=1, source_target_pairs={{0,7},{1,8},{2,9},{3,10},{4,11},{5,12},{6,13},{7,14},{8,15},{9,16}... | collective-permute-start | bytes 9224
  289.5 21.6 %collective-permute-start.41 = (bf16[192,8]{0,1:T(8,128)(2,1)S(1)}, bf16[192,8]{0,1:T(8,128)(2,1)S(1)}, u32[]{:S(2)}, u32[]{:S(2)}) collective-permute-start(bf16[192,8]{0,1:T(8,128)(2,1)S(1)} %get-tuple-element.38), channel_id=1, source_target_pairs={{0,6},{1,7},{2,8},{3,9},{4,10},{5,11},{6,12},{7,13},{8,14},{9,15},... | collective-permute-start | bytes 9224
  291.4 21.8 %collective-permute-start.40 = (bf16[192,8]{0,1:T(8,128)(2,1)S(1)}, bf16[192,8]{0,1:T(8,128)(2,1)S(1)}, u32[]{:S(2)}, u32[]{:S(2)}) collective-permute-start(bf16[192,8]{0,1:T(8,128)(2,1)S(1)} %get-tuple-element.38), channel_id=1, source_target_pairs={{0,5},{1,6},{2,7},{3,8},{4,9},{5,10},{6,11},{7,12},{8,13},{9,14},{... | collective-permute-start | bytes 9224
  302.3 15.1 %collective-permute-start.39 = (bf16[192,8]{0,1:T(8,128)(2,1)S(1)}, bf16[192,8]{0,1:T(8,128)(2,1)S(1)}, u32[]{:S(2)}, u32[]{:S(2)}) collective-permute-start(bf16[192,8]{0,1:T(8,128)(2,1)S(1)} %get-tuple-element.38), channel_id=1, source_target_pairs={{0,4},{1,5},{2,6},{3,7},{4,8},{5,9},{6,10},{7,11},{8,12},{9,13},{1... | collective-permute-start | bytes 9224
  304.3 15.1 %collective-permute-start.38 = (bf16[192,8]{0,1:T(8,128)(2,1)S(1)}, bf16[192,8]{0,1:T(8,128)(2,1)S(1)}, u32[]{:S(2)}, u32[]{:S(2)}) collective-permute-start(bf16[192,8]{0,1:T(8,128)(2,1)S(1)} %get-tuple-element.38), channel_id=1, source_target_pairs={{0,3},{1,4},{2,5},{3,6},{4,7},{5,8},{6,9},{7,10},{8,11},{9,12},{10... | collective-permute-start | bytes 9224
  308.9 117.0 %collective-permute-start.37 = (bf16[192,8]{0,1:T(8,128)(2,1)S(1)}, bf16[192,8]{0,1:T(8,128)(2,1)S(1)}, u32[]{:S(2)}, u32[]{:S(2)}) collective-permute-start(bf16[192,8]{0,1:T(8,128)(2,1)S(1)} %get-tuple-element.38), channel_id=1, source_target_pairs={{0,2},{1,3},{2,4},{3,5},{4,6},{5,7},{6,8},{7,9},{8,10},{9,11},{10,... | collective-permute-start | bytes 9224
  311.1 118.1 %collective-permute-start.36 = (bf16[192,8]{0,1:T(8,128)(2,1)S(1)}, bf16[192,8]{0,1:T(8,128)(2,1)S(1)}, u32[]{:S(2)}, u32[]{:S(2)}) collective-permute-start(bf16[192,8]{0,1:T(8,128)(2,1)S(1)} %get-tuple-element.38), channel_id=1, source_target_pairs={{0,1},{1,2},{2,3},{3,4},{4,5},{5,6},{6,7},{7,8},{8,9},{9,10},{10,1... | collective-permute-start | bytes 9224
  313.2 117.9 %collective-permute-start.34 = (bf16[192,8]{0,1:T(8,128)(2,1)S(1)}, bf16[192,8]{0,1:T(8,128)(2,1)S(1)}, u32[]{:S(2)}, u32[]{:S(2)}) collective-permute-start(bf16[192,8]{0,1:T(8,128)(2,1)S(1)} %get-tuple-element.39), channel_id=1, source_target_pairs={{0,7},{1,8},{2,9},{3,10},{4,11},{5,12},{6,13},{7,14},{8,15},{9,16}... | collective-permute-start | bytes 9224
  317.5 118.5 %collective-permute-start.33 = (bf16[192,8]{0,1:T(8,128)(2,1)S(1)}, bf16[192,8]{0,1:T(8,128)(2,1)S(1)}, u32[]{:S(2)}, u32[]{:S(2)}) collective-permute-start(bf16[192,8]{0,1:T(8,128)(2,1)S(1)} %get-tuple-element.39), channel_id=1, source_target_pairs={{0,6},{1,7},{2,8},{3,9},{4,10},{5,11},{6,12},{7,13},{8,14},{9,15},... | collective-permute-start | bytes 9224
  319.4 118.5 %collective-permute-start.32 = (bf16[192,8]{0,1:T(8,128)(2,1)S(1)}, bf16[192,8]{0,1:T(8,128)(2,1)S(1)}, u32[]{:S(2)}, u32[]{:S(2)}) collective-permute-start(bf16[192,8]{0,1:T(8,128)(2,1)S(1)} %get-tuple-element.39), channel_id=1, source_target_pairs={{0,5},{1,6},{2,7},{3,8},{4,9},{5,10},{6,11},{7,12},{8,13},{9,14},{... | collective-permute-start | bytes 9224
  426.0 17.8 %collective-permute-start.31 = (bf16[192,8]{0,1:T(8,128)(2,1)S(1)}, bf16[192,8]{0,1:T(8,128)(2,1)S(1)}, u32[]{:S(2)}, u32[]{:S(2)}) collective-permute-start(bf16[192,8]{0,1:T(8,128)(2,1)S(1)} %get-tuple-element.39), channel_id=1, source_target_pairs={{0,4},{1,5},{2,6},{3,7},{4,8},{5,9},{6,10},{7,11},{8,12},{9,13},{1... | collective-permute-start | bytes 9224
  429.2 20.1 %collective-permute-start.30 = (bf16[192,8]{0,1:T(8,128)(2,1)S(1)}, bf16[192,8]{0,1:T(8,128)(2,1)S(1)}, u32[]{:S(2)}, u32[]{:S(2)}) collective-permute-start(bf16[192,8]{0,1:T(8,128)(2,1)S(1)} %get-tuple-element.39), channel_id=1, source_target_pairs={{0,3},{1,4},{2,5},{3,6},{4,7},{5,8},{6,9},{7,10},{8,11},{9,12},{10... | collective-permute-start | bytes 9224
  431.1 22.2 %collective-permute-start.29 = (bf16[192,8]{0,1:T(8,128)(2,1)S(1)}, bf16[192,8]{0,1:T(8,128)(2,1)S(1)}, u32[]{:S(2)}, u32[]{:S(2)}) collective-permute-start(bf16[192,8]{0,1:T(8,128)(2,1)S(1)} %get-tuple-element.39), channel_id=1, source_target_pairs={{0,2},{1,3},{2,4},{3,5},{4,6},{5,7},{6,8},{7,9},{8,10},{9,11},{10,... | collective-permute-start | bytes 9224
  435.9 19.3 %collective-permute-start.28 = (bf16[192,8]{0,1:T(8,128)(2,1)S(1)}, bf16[192,8]{0,1:T(8,128)(2,1)S(1)}, u32[]{:S(2)}, u32[]{:S(2)}) collective-permute-start(bf16[192,8]{0,1:T(8,128)(2,1)S(1)} %get-tuple-element.39), channel_id=1, source_target_pairs={{0,1},{1,2},{2,3},{3,4},{4,5},{5,6},{6,7},{7,8},{8,9},{9,10},{10,1... | collective-permute-start | bytes 9224
  437.9 19.3 %collective-permute-start.27 = (bf16[192,18]{0,1:T(8,128)(2,1)S(1)}, bf16[192,18]{0,1:T(8,128)(2,1)S(1)}, u32[]{:S(2)}, u32[]{:S(2)}) collective-permute-start(bf16[192,18]{0,1:T(8,128)(2,1)S(1)} %slice.209), channel_id=1, source_target_pairs={{0,8},{1,9},{2,10},{3,11},{4,12},{5,13},{6,14},{7,15},{8,16},{9,17... | collective-permute-start | bytes 20744
  443.7 17.1 %collective-permute-start.26 = (bf16[192,24]{0,1:T(8,128)(2,1)S(1)}, bf16[192,24]{0,1:T(8,128)(2,1)S(1)}, u32[]{:S(2)}, u32[]{:S(2)}) collective-permute-start(bf16[192,24]{0,1:T(8,128)(2,1)S(1)} %get-tuple-element.36), channel_id=1, source_target_pairs={{0,7},{1,8},{2,9},{3,10},{4,11},{5,12},{6,13},{7,14},{8,15},{9,16}... | collective-permute-start | bytes 27656
  (104 other events, 1225.3 us)
Sparse Core Ops, SparseCore 0:
  278.2 76.3 reduce-scatter.30
  357.3 69.7 reduce-scatter.32
  431.8 114.0 reduce-scatter.28
  550.3 116.8 reduce-scatter.26
where the time goes:
time: 751 us; the launch traced here: 741 us
  blocking collectives  237 us (32%)
  waiting for transfers between devices  193 us (26%)
  starting transfers between devices  182 us (24%)
  local copies, waits for them, and re-layouts  55.5 us (7%)
  matrix products  40.7 us (5%)
  between operations  18.5 us (2%)
  other arithmetic  14.1 us (2%)
    reduce_scatter x2, waiting for transfers between devices, reduce_grads(): lax.psum_scatter(inner_term.astype(jnp.bfloat16), 'cols', scatter_dimensi...  173 us
    unnamed x50, starting transfers between devices  139 us
    unnamed x2, blocking collectives  133 us
    psum x1, blocking collectives, local(): table_sum = lax.psum(jnp.stack([table_one, table_two]), ('rows', 'cols'))  105 us
    ppermute x6, starting transfers between devices, with_halo(): lax.ppermute(lax.slice_in_dim(block, block.shape[dim] - width, None, axis...  24 us
    unnamed x173, local copies, waits for them, and re-layouts  19 us
    ppermute x6, starting transfers between devices, with_halo(): lax.ppermute(lax.slice_in_dim(block, 0, width, axis=dim), axis, backward)  18.5 us
  transfers between devices with their start and end apart: 64, of which 13 were waited for; matrix products, arithmetic and copies ran while one was open for 6% of the time, Pallas kernels for 0%

commit v1 on v0

--- a/solution.py
+++ b/solution.py
@@ -376,7 +376,7 @@
         grad_mid_one.reshape(tile_rows, tile_cols, channels).astype(jnp.float32) + grad_tokens
     ).astype(jnp.bfloat16)
     summed_one = reduce_grads(qkv_one_grad, proj_one, inner_one, outer_one)
-    table_sum = lax.psum(jnp.stack([table_one, table_two]), ("rows", "cols"))
+    table_sum = lax.psum(lax.psum(jnp.stack([table_one, table_two]), "cols"), "rows")
     qkv_grad = jnp.stack([summed_one[0], summed_two[0]])
     proj_grad = jnp.stack([summed_one[1], summed_two[1]])
     inner_grad = jnp.stack([summed_one[2], summed_two[2]])

time: 751 us -> 750 us (level)
  waiting for transfers between devices: 193 us -> 111 us
  blocking collectives: 237 us -> 310 us
  starting transfers between devices: 182 us -> 191 us
    reduce_scatter x2, waiting for transfers between devices: 173 us -> 89.8 us  [reduce_grads(): lax.psum_scatter(inner_term.astype(jnp.bfloat16), 'cols', scatter_dimensi...]
    psum x1 -> x2, blocking collectives: 105 us -> 177 us  [the longest x1 114 us: local(): lax.psum(jnp.stack([table_one, table_two]), 'cols')]
    unnamed x50, starting transfers between devices: 139 us -> 148 us
  transfers between devices with their start and end apart: 64 -> 64, of which waited for: 13 -> 12; matrix products, arithmetic and copies ran while one was open for 6% -> 6% of each run, Pallas kernels for 0% -> 0%
where the time goes in v1:
time: 750 us; the launch traced here: 740 us
  blocking collectives  310 us (41%)
  starting transfers between devices  191 us (25%)
  waiting for transfers between devices  111 us (15%)
  local copies, waits for them, and re-layouts  55.4 us (7%)
  matrix products  40.7 us (5%)
  between operations  18.5 us (2%)
  other arithmetic  13.5 us (2%)
    unnamed x50, starting transfers between devices  148 us
    unnamed x2, blocking collectives  133 us
    psum x1, blocking collectives, local(): lax.psum(jnp.stack([table_one, table_two]), 'cols')  114 us
    reduce_scatter x2, waiting for transfers between devices, reduce_grads(): lax.psum_scatter(inner_term.astype(jnp.bfloat16), 'cols', scatter_dimensi...  89.8 us
    psum x1, blocking collectives, local(): lax.psum(lax.psum(jnp.stack([table_one, table_two]), 'cols'), 'rows')  63.8 us
    ppermute x6, starting transfers between devices, with_halo(): lax.ppermute(lax.slice_in_dim(block, block.shape[dim] - width, None, axis...  23.3 us
    unnamed x173, local copies, waits for them, and re-layouts  20.1 us
    ppermute x6, starting transfers between devices, with_halo(): lax.ppermute(lax.slice_in_dim(block, 0, width, axis=dim), axis, backward)  18.5 us
  transfers between devices with their start and end apart: 64, of which 12 were waited for; matrix products, arithmetic and copies ran while one was open for 6% of the time, Pallas kernels for 0%

profile of v1, /device:TPU:16, one launch (start us, length us, event | category | flops | bytes accessed | tf_op | source)
XLA Modules:
  0.0 739.6 jit_solution(2043835094992381282)
XLA Ops:
  8.0 4.3 collective-permute-start.4
  26.2 2.9 multiply_convert_fusion.1
  31.8 5.5 collective-permute-start
  42.9 6.0 collective-permute-start.7
  50.8 4.1 collective-permute-start.2
  55.0 3.9 collective-permute-start.3
  63.6 3.2 reshape.352
  93.3 4.1 copy.147
  97.4 5.6 convert_element_type.304
  114.4 3.2 collective-permute-start.8
  117.6 4.7 collective-permute-start.9
  124.2 4.3 collective-permute-start.10
  130.6 6.0 collective-permute-done.11
  144.8 68.5 %fusion.122 = (bf16[192,24]{0,1:T(8,128)(2,1)S(1)}, bf16[192,24]{0,1:T(8,128)(2,1)S(1)}, bf16[192,8]{0,1:T(8,128)(2,1)S(1)}, bf16[192,8]{0,1:T(8,128)(2,1)S(1)},...) fusion(bf16[192,576]{0,1:T(8,128)(2,1)} %convolution_convert_fusion.9, ...), kind=kCustom, calls=%all-reduce-scatter.6 | all-reduce-scatter fusion | flops 786434 | bytes 1230848
  213.4 20.4 %collective-permute-start.51 = (bf16[768,6]{0,1:T(8,128)(2,1)S(1)}, bf16[768,6]{0,1:T(8,128)(2,1)S(1)}, u32[]{:S(2)}, u32[]{:S(2)}) collective-permute-start(bf16[768,6]{0,1:T(8,128)(2,1)S(1)} %slice.212), channel_id=1, source_target_pairs={{0,8},{1,9},{2,10},{3,11},{4,12},{5,13},{6,14},{7,15},{8,16},{9,17... | collective-permute-start | bytes 27656
  241.5 4.6 collective-permute-start.46
  267.3 3.1 collective-permute-start.54
  270.5 3.3 collective-permute-start.53
  302.9 4.6 collective-permute-start.38
  307.5 113.6 %psum.14 = f32[2,225,6]{1,2,0:T(8,128)S(1)} all-reduce(f32[2,225,6]{1,2,0:T(8,128)S(1)} %pad_maximum_fusion.16), channel_id=1, replica_groups=mesh['rows'=16,'cols'=32] {'cols'}, use_global_device_ids=true, to_apply=%region_40.41 | all-reduce | flops 2700 | bytes 21600 | tf_op jit(solution)/shard_map/psum | solution.py:379
  421.1 6.8 collective-permute-start.37
  427.9 4.0 collective-permute-start.36
  431.8 15.1 %collective-permute-start.34 = (bf16[192,8]{0,1:T(8,128)(2,1)S(1)}, bf16[192,8]{0,1:T(8,128)(2,1)S(1)}, u32[]{:S(2)}, u32[]{:S(2)}) collective-permute-start(bf16[192,8]{0,1:T(8,128)(2,1)S(1)} %get-tuple-element.39), channel_id=1, source_target_pairs={{0,7},{1,8},{2,9},{3,10},{4,11},{5,12},{6,13},{7,14},{8,15},{9,16}... | collective-permute-start | bytes 9224
  451.4 63.8 %psum.15 = f32[2,225,6]{1,2,0:T(8,128)S(1)} all-reduce(f32[2,225,6]{1,2,0:T(8,128)S(1)} %psum.14), channel_id=1, replica_groups=mesh['rows'=16,'cols'=32] {'rows'}, use_global_device_ids=true, to_apply=%region_41.42 | all-reduce | flops 2700 | bytes 21600 | tf_op jit(solution)/shard_map/psum | solution.py:379
  519.1 4.0 collective-permute-start.29
  528.5 3.6 collective-permute-start.26
  537.9 2.9 collective-permute-start.22
  541.7 3.6 collective-permute-start.21
  561.8 3.6 collective-permute-start.13
  569.8 3.0 collective-permute-done.12
  576.2 89.8 %reduce-scatter.27.cloned.1.call-done = bf16[192,24]{0,1:T(8,128)(2,1)} async-done(((bf16[192,768]{0,1:T(8,128)(2,1)}), bf16[192,24]{0,1:T(8,128)(2,1)}) %reduce-scatter.27.cloned.1.call-update) | async-done | bytes 9232 | tf_op jit(solution)/shard_map/reduce_scatter | solution.py:241
  666.0 64.4 %all-reduce.19 = (bf16[192,18]{0,1:T(8,128)(2,1)S(1)}, bf16[192,18]{0,1:T(8,128)(2,1)S(1)}, bf16[192,6]{0,1:T(8,128)(2,1)S(1)}, bf16[192,6]{0,1:T(8,128)(2,1)S(1...) all-reduce(bf16[192,18]{0,1:T(8,128)(2,1)S(1)} %constant_dynamic-sl, ...), channel_id=5, replica_groups=mesh['rows'=16,'cols'=32] {'rows'}, use_global_device_ids=true, to_apply=%region_25.26.clone | all-reduce | flops 18432 | bytes 73728
  (449 shorter events, 180.5 us)
Async XLA Ops:
  7.2 566.8 %reduce-scatter.31.cloned.1.call-start = ((), (), s32[]{:S(2)}) async-start(), calls=%async_computation.6 | async-start | bytes 208896
  8.0 32.9 %collective-permute-start.4 = (bf16[4,32]{1,0:T(4,128)(2,1)S(1)}, bf16[4,32]{1,0:T(4,128)(2,1)S(1)}, u32[]{:S(2)}, u32[]{:S(2)}) collective-permute-start(bf16[4,32]{1,0:T(4,128)(2,1)S(1)} %get-tuple-element.76), channel_id=1, source_target_pairs={{0,32},{32,64},{64,96},{96,128},{128,160},{160,192},{192,224},{224... | collective-permute-start | bytes 776 | tf_op jit(solution)/shard_map/ppermute | solution.py:20
  12.2 28.6 %collective-permute-start.5 = (bf16[4,32]{1,0:T(4,128)(2,1)S(1)}, bf16[4,32]{1,0:T(4,128)(2,1)S(1)}, u32[]{:S(2)}, u32[]{:S(2)}) collective-permute-start(bf16[4,32]{1,0:T(4,128)(2,1)S(1)} %get-tuple-element.77), channel_id=1, source_target_pairs={{32,0},{64,32},{96,64},{128,96},{160,128},{192,160},{224,192},{256... | collective-permute-start | bytes 776 | tf_op jit(solution)/shard_map/ppermute | solution.py:23
  30.4 20.3 %collective-permute-start.1 = (bf16[4,32,192]{2,1,0:T(8,128)(2,1)S(1)}, bf16[4,32,192]{2,1,0:T(8,128)(2,1)S(1)}, u32[]{:S(2)}, u32[]{:S(2)}) collective-permute-start(bf16[4,32,192]{2,1,0:T(8,128)(2,1)S(1)} %bitcast.340), channel_id=1, source_target_pairs={{32,0},{64,32},{96,64},{128,96},{160,128},{192,160},{224,192},{256... | collective-permute-start | bytes 147464 | tf_op jit(solution)/shard_map/ppermute | solution.py:23
  31.8 18.9 %collective-permute-start = (bf16[4,32,192]{2,1,0:T(8,128)(2,1)S(1)}, bf16[4,32,192]{2,1,0:T(8,128)(2,1)S(1)}, u32[]{:S(2)}, u32[]{:S(2)}) collective-permute-start(bf16[4,32,192]{2,1,0:T(8,128)(2,1)S(1)} %bitcast.341), channel_id=1, source_target_pairs={{0,32},{32,64},{64,96},{96,128},{128,160},{160,192},{192,224},{224... | collective-permute-start | bytes 147464 | tf_op jit(solution)/shard_map/ppermute | solution.py:20
  213.4 28.1 %collective-permute-start.51 = (bf16[768,6]{0,1:T(8,128)(2,1)S(1)}, bf16[768,6]{0,1:T(8,128)(2,1)S(1)}, u32[]{:S(2)}, u32[]{:S(2)}) collective-permute-start(bf16[768,6]{0,1:T(8,128)(2,1)S(1)} %slice.212), channel_id=1, source_target_pairs={{0,8},{1,9},{2,10},{3,11},{4,12},{5,13},{6,14},{7,15},{8,16},{9,17... | collective-permute-start | bytes 27656
  233.8 16.9 %collective-permute-start.50 = (bf16[768,8]{0,1:T(8,128)(2,1)S(1)}, bf16[768,8]{0,1:T(8,128)(2,1)S(1)}, u32[]{:S(2)}, u32[]{:S(2)}) collective-permute-start(bf16[768,8]{0,1:T(8,128)(2,1)S(1)} %get-tuple-element.41), channel_id=1, source_target_pairs={{0,7},{1,8},{2,9},{3,10},{4,11},{5,12},{6,13},{7,14},{8,15},{9,16}... | collective-permute-start | bytes 36872
  235.7 16.9 %collective-permute-start.49 = (bf16[768,8]{0,1:T(8,128)(2,1)S(1)}, bf16[768,8]{0,1:T(8,128)(2,1)S(1)}, u32[]{:S(2)}, u32[]{:S(2)}) collective-permute-start(bf16[768,8]{0,1:T(8,128)(2,1)S(1)} %get-tuple-element.41), channel_id=1, source_target_pairs={{0,6},{1,7},{2,8},{3,9},{4,10},{5,11},{6,12},{7,13},{8,14},{9,15},... | collective-permute-start | bytes 36872
  237.7 16.9 %collective-permute-start.48 = (bf16[768,8]{0,1:T(8,128)(2,1)S(1)}, bf16[768,8]{0,1:T(8,128)(2,1)S(1)}, u32[]{:S(2)}, u32[]{:S(2)}) collective-permute-start(bf16[768,8]{0,1:T(8,128)(2,1)S(1)} %get-tuple-element.41), channel_id=1, source_target_pairs={{0,5},{1,6},{2,7},{3,8},{4,9},{5,10},{6,11},{7,12},{8,13},{9,14},{... | collective-permute-start | bytes 36872
  239.6 17.2 %collective-permute-start.47 = (bf16[768,8]{0,1:T(8,128)(2,1)S(1)}, bf16[768,8]{0,1:T(8,128)(2,1)S(1)}, u32[]{:S(2)}, u32[]{:S(2)}) collective-permute-start(bf16[768,8]{0,1:T(8,128)(2,1)S(1)} %get-tuple-element.41), channel_id=1, source_target_pairs={{0,4},{1,5},{2,6},{3,7},{4,8},{5,9},{6,10},{7,11},{8,12},{9,13},{1... | collective-permute-start | bytes 36872
  241.5 17.2 %collective-permute-start.46 = (bf16[768,8]{0,1:T(8,128)(2,1)S(1)}, bf16[768,8]{0,1:T(8,128)(2,1)S(1)}, u32[]{:S(2)}, u32[]{:S(2)}) collective-permute-start(bf16[768,8]{0,1:T(8,128)(2,1)S(1)} %get-tuple-element.41), channel_id=1, source_target_pairs={{0,3},{1,4},{2,5},{3,6},{4,7},{5,8},{6,9},{7,10},{8,11},{9,12},{10... | collective-permute-start | bytes 36872
  250.7 19.8 %collective-permute-start.58 = (bf16[768,8]{0,1:T(8,128)(2,1)S(1)}, bf16[768,8]{0,1:T(8,128)(2,1)S(1)}, u32[]{:S(2)}, u32[]{:S(2)}) collective-permute-start(bf16[768,8]{0,1:T(8,128)(2,1)S(1)} %get-tuple-element.40), channel_id=1, source_target_pairs={{0,7},{1,8},{2,9},{3,10},{4,11},{5,12},{6,13},{7,14},{8,15},{9,16}... | collective-permute-start | bytes 36872
  252.6 21.2 %collective-permute-start.57 = (bf16[768,8]{0,1:T(8,128)(2,1)S(1)}, bf16[768,8]{0,1:T(8,128)(2,1)S(1)}, u32[]{:S(2)}, u32[]{:S(2)}) collective-permute-start(bf16[768,8]{0,1:T(8,128)(2,1)S(1)} %get-tuple-element.40), channel_id=1, source_target_pairs={{0,6},{1,7},{2,8},{3,9},{4,10},{5,11},{6,12},{7,13},{8,14},{9,15},... | collective-permute-start | bytes 36872
  262.5 14.2 %collective-permute-start.56 = (bf16[768,8]{0,1:T(8,128)(2,1)S(1)}, bf16[768,8]{0,1:T(8,128)(2,1)S(1)}, u32[]{:S(2)}, u32[]{:S(2)}) collective-permute-start(bf16[768,8]{0,1:T(8,128)(2,1)S(1)} %get-tuple-element.40), channel_id=1, source_target_pairs={{0,5},{1,6},{2,7},{3,8},{4,9},{5,10},{6,11},{7,12},{8,13},{9,14},{... | collective-permute-start | bytes 36872
  276.6 298.1 %reduce-scatter.33.cloned.1.call-start = ((), (), s32[]{:S(2)}) async-start(), calls=%async_computation.7 | async-start | bytes 208896
  283.1 293.1 %reduce-scatter.29.cloned.1.call-start = ((), (), s32[]{:S(2)}) async-start(), calls=%async_computation.5 | async-start | bytes 405504 | tf_op jit(solution)/shard_map/reduce_scatter | solution.py:241
  284.8 381.2 %reduce-scatter.27.cloned.1.call-start = ((), (), s32[]{:S(2)}) async-start(), calls=%async_computation.4 | async-start | bytes 405504 | tf_op jit(solution)/shard_map/reduce_scatter | solution.py:241
  286.0 135.0 %collective-permute-start.42 = (bf16[192,8]{0,1:T(8,128)(2,1)S(1)}, bf16[192,8]{0,1:T(8,128)(2,1)S(1)}, u32[]{:S(2)}, u32[]{:S(2)}) collective-permute-start(bf16[192,8]{0,1:T(8,128)(2,1)S(1)} %get-tuple-element.38), channel_id=1, source_target_pairs={{0,7},{1,8},{2,9},{3,10},{4,11},{5,12},{6,13},{7,14},{8,15},{9,16}... | collective-permute-start | bytes 9224
  288.1 139.7 %collective-permute-start.41 = (bf16[192,8]{0,1:T(8,128)(2,1)S(1)}, bf16[192,8]{0,1:T(8,128)(2,1)S(1)}, u32[]{:S(2)}, u32[]{:S(2)}) collective-permute-start(bf16[192,8]{0,1:T(8,128)(2,1)S(1)} %get-tuple-element.38), channel_id=1, source_target_pairs={{0,6},{1,7},{2,8},{3,9},{4,10},{5,11},{6,12},{7,13},{8,14},{9,15},... | collective-permute-start | bytes 9224
  290.0 141.8 %collective-permute-start.40 = (bf16[192,8]{0,1:T(8,128)(2,1)S(1)}, bf16[192,8]{0,1:T(8,128)(2,1)S(1)}, u32[]{:S(2)}, u32[]{:S(2)}) collective-permute-start(bf16[192,8]{0,1:T(8,128)(2,1)S(1)} %get-tuple-element.38), channel_id=1, source_target_pairs={{0,5},{1,6},{2,7},{3,8},{4,9},{5,10},{6,11},{7,12},{8,13},{9,14},{... | collective-permute-start | bytes 9224
  301.0 146.0 %collective-permute-start.39 = (bf16[192,8]{0,1:T(8,128)(2,1)S(1)}, bf16[192,8]{0,1:T(8,128)(2,1)S(1)}, u32[]{:S(2)}, u32[]{:S(2)}) collective-permute-start(bf16[192,8]{0,1:T(8,128)(2,1)S(1)} %get-tuple-element.38), channel_id=1, source_target_pairs={{0,4},{1,5},{2,6},{3,7},{4,8},{5,9},{6,10},{7,11},{8,12},{9,13},{1... | collective-permute-start | bytes 9224
  302.9 146.3 %collective-permute-start.38 = (bf16[192,8]{0,1:T(8,128)(2,1)S(1)}, bf16[192,8]{0,1:T(8,128)(2,1)S(1)}, u32[]{:S(2)}, u32[]{:S(2)}) collective-permute-start(bf16[192,8]{0,1:T(8,128)(2,1)S(1)} %get-tuple-element.38), channel_id=1, source_target_pairs={{0,3},{1,4},{2,5},{3,6},{4,7},{5,8},{6,9},{7,10},{8,11},{9,12},{10... | collective-permute-start | bytes 9224
  421.1 94.2 %collective-permute-start.37 = (bf16[192,8]{0,1:T(8,128)(2,1)S(1)}, bf16[192,8]{0,1:T(8,128)(2,1)S(1)}, u32[]{:S(2)}, u32[]{:S(2)}) collective-permute-start(bf16[192,8]{0,1:T(8,128)(2,1)S(1)} %get-tuple-element.38), channel_id=1, source_target_pairs={{0,2},{1,3},{2,4},{3,5},{4,6},{5,7},{6,8},{7,9},{8,10},{9,11},{10,... | collective-permute-start | bytes 9224
  427.9 89.3 %collective-permute-start.36 = (bf16[192,8]{0,1:T(8,128)(2,1)S(1)}, bf16[192,8]{0,1:T(8,128)(2,1)S(1)}, u32[]{:S(2)}, u32[]{:S(2)}) collective-permute-start(bf16[192,8]{0,1:T(8,128)(2,1)S(1)} %get-tuple-element.38), channel_id=1, source_target_pairs={{0,1},{1,2},{2,3},{3,4},{4,5},{5,6},{6,7},{7,8},{8,9},{9,10},{10,1... | collective-permute-start | bytes 9224
  431.8 87.3 %collective-permute-start.34 = (bf16[192,8]{0,1:T(8,128)(2,1)S(1)}, bf16[192,8]{0,1:T(8,128)(2,1)S(1)}, u32[]{:S(2)}, u32[]{:S(2)}) collective-permute-start(bf16[192,8]{0,1:T(8,128)(2,1)S(1)} %get-tuple-element.39), channel_id=1, source_target_pairs={{0,7},{1,8},{2,9},{3,10},{4,11},{5,12},{6,13},{7,14},{8,15},{9,16}... | collective-permute-start | bytes 9224
  447.0 76.2 %collective-permute-start.33 = (bf16[192,8]{0,1:T(8,128)(2,1)S(1)}, bf16[192,8]{0,1:T(8,128)(2,1)S(1)}, u32[]{:S(2)}, u32[]{:S(2)}) collective-permute-start(bf16[192,8]{0,1:T(8,128)(2,1)S(1)} %get-tuple-element.39), channel_id=1, source_target_pairs={{0,6},{1,7},{2,8},{3,9},{4,10},{5,11},{6,12},{7,13},{8,14},{9,15},... | collective-permute-start | bytes 9224
  449.2 75.9 %collective-permute-start.32 = (bf16[192,8]{0,1:T(8,128)(2,1)S(1)}, bf16[192,8]{0,1:T(8,128)(2,1)S(1)}, u32[]{:S(2)}, u32[]{:S(2)}) collective-permute-start(bf16[192,8]{0,1:T(8,128)(2,1)S(1)} %get-tuple-element.39), channel_id=1, source_target_pairs={{0,5},{1,6},{2,7},{3,8},{4,9},{5,10},{6,11},{7,12},{8,13},{9,14},{... | collective-permute-start | bytes 9224
  517.2 14.9 %collective-permute-start.30 = (bf16[192,8]{0,1:T(8,128)(2,1)S(1)}, bf16[192,8]{0,1:T(8,128)(2,1)S(1)}, u32[]{:S(2)}, u32[]{:S(2)}) collective-permute-start(bf16[192,8]{0,1:T(8,128)(2,1)S(1)} %get-tuple-element.39), channel_id=1, source_target_pairs={{0,3},{1,4},{2,5},{3,6},{4,7},{5,8},{6,9},{7,10},{8,11},{9,12},{10... | collective-permute-start | bytes 9224
  519.1 14.9 %collective-permute-start.29 = (bf16[192,8]{0,1:T(8,128)(2,1)S(1)}, bf16[192,8]{0,1:T(8,128)(2,1)S(1)}, u32[]{:S(2)}, u32[]{:S(2)}) collective-permute-start(bf16[192,8]{0,1:T(8,128)(2,1)S(1)} %get-tuple-element.39), channel_id=1, source_target_pairs={{0,2},{1,3},{2,4},{3,5},{4,6},{5,7},{6,8},{7,9},{8,10},{9,11},{10,... | collective-permute-start | bytes 9224
  547.2 14.6 %collective-permute-start.18 = (bf16[192,24]{0,1:T(8,128)(2,1)S(1)}, bf16[192,24]{0,1:T(8,128)(2,1)S(1)}, u32[]{:S(2)}, u32[]{:S(2)}) collective-permute-start(bf16[192,24]{0,1:T(8,128)(2,1)S(1)} %get-tuple-element.37), channel_id=1, source_target_pairs={{0,7},{1,8},{2,9},{3,10},{4,11},{5,12},{6,13},{7,14},{8,15},{9,16}... | collective-permute-start | bytes 27656
  549.1 16.3 %collective-permute-start.17 = (bf16[192,24]{0,1:T(8,128)(2,1)S(1)}, bf16[192,24]{0,1:T(8,128)(2,1)S(1)}, u32[]{:S(2)}, u32[]{:S(2)}) collective-permute-start(bf16[192,24]{0,1:T(8,128)(2,1)S(1)} %get-tuple-element.37), channel_id=1, source_target_pairs={{0,6},{1,7},{2,8},{3,9},{4,10},{5,11},{6,12},{7,13},{8,14},{9,15},... | collective-permute-start | bytes 27656
  553.3 14.1 %collective-permute-start.16 = (bf16[192,24]{0,1:T(8,128)(2,1)S(1)}, bf16[192,24]{0,1:T(8,128)(2,1)S(1)}, u32[]{:S(2)}, u32[]{:S(2)}) collective-permute-start(bf16[192,24]{0,1:T(8,128)(2,1)S(1)} %get-tuple-element.37), channel_id=1, source_target_pairs={{0,5},{1,6},{2,7},{3,8},{4,9},{5,10},{6,11},{7,12},{8,13},{9,14},{... | collective-permute-start | bytes 27656
  (104 other events, 1189.9 us)
Sparse Core Ops, SparseCore 0:
  276.8 76.2 reduce-scatter.30
  355.8 69.9 reduce-scatter.32
  430.4 114.2 reduce-scatter.28
  549.1 116.8 reduce-scatter.26
